TPU v7x, 128 devices: a whole 4x4x4 slice. The times are simulated.
128 devices in a mesh: row: 16 (over z_lo, y, core), col: 8 (over x, z_hi).
Axes of the slice: x: 4, y: 4, z: 4 (z_hi: 2, z_lo: 2; z = z_hi * 2 + z_lo), core: 2. Of those that a mesh axis runs over, the one named last changes fastest.
Arguments:
- pair: bfloat16 [1024, 1024, 128], P('row', 'col'), may hold values from -6 to 6
- ln_gain: float32 [128], replicated, may hold values from 0.1 to 1.9
- ln_bias: float32 [128], replicated, may hold values from -3 to 3
- gate_weight: bfloat16 [128, 512], replicated, may hold values from -0.5 to 0.5
- up_weight: bfloat16 [128, 512], replicated, may hold values from -0.5 to 0.5
- out_weight: bfloat16 [512, 128], replicated, may hold values from -0.25 to 0.25
- head_weight: bfloat16 [128, 64], replicated, may hold values from -1 to 1
- targets: int32 [1024, 1024], P(('row', 'col')), may hold values from 0 to 63
- pair_mask: int32 [1024, 1024], P(('row', 'col')), may hold values 0 or 1
Outputs:
- pair_out: bfloat16 [1024, 1024, 128], P('row', 'col')
- loss: float32 [], replicated
- grad_gain: float32 [128], replicated
- grad_bias: float32 [128], replicated
- grad_gate: float32 [128, 512], replicated
- grad_up: float32 [128, 512], replicated
- grad_out: float32 [512, 128], replicated
- grad_head: float32 [128, 64], replicated
All inputs are finite; a program needn't handle non-finite values. No bound on the sum of `pair_mask` on one device may be relied on, other than what follows from the above.
Results may differ from a plain program's by a relative error of at most 0.001.
The roundings to bfloat16 on the way count: a program that leaves them out, or rounds other values in their place, can miss the bound.
Values may be sent and summed in bfloat16 or wider, within the bound.
No kernel may reach another device: no remote copies, remote signals or barrier semaphores. Data moves between devices by JAX's collectives and lax.ppermute only.
A program may use at most 64 MiB of HBM per device.

v0:
```python
import math
import jax
import jax.numpy as jnp
from jax import lax
from jax.sharding import PartitionSpec as P

EPSILON = 1e-05


def normalize(rows_in, ln_gain, ln_bias):
    values = rows_in.astype(jnp.float32)
    centered = values - jnp.mean(values, axis=-1, keepdims=True)
    variance = jnp.mean(centered * centered, axis=-1, keepdims=True)
    unit_rows = centered * lax.rsqrt(variance + EPSILON)
    normed = (unit_rows * ln_gain + ln_bias).astype(jnp.bfloat16)
    return (unit_rows, normed)


def inner(left, right):
    return lax.dot_general(
        left, right, (((0,), (0,)), ((), ())), preferred_element_type=jnp.float32
    )


def advance(rows_in, ln_gain, ln_bias, gate_weight, up_weight, out_weight):
    unit_rows, normed = normalize(rows_in, ln_gain, ln_bias)
    gate_pre = jnp.dot(normed, gate_weight, preferred_element_type=jnp.float32)
    up_pre = jnp.dot(normed, up_weight, preferred_element_type=jnp.float32)
    hidden = (jax.nn.silu(gate_pre) * up_pre).astype(jnp.bfloat16)
    update = jnp.dot(hidden, out_weight, preferred_element_type=jnp.float32)
    return (rows_in.astype(jnp.float32) + update).astype(jnp.bfloat16)


def retreat(totals, rows_in, grad_rows, ln_gain, ln_bias, gate_weight, up_weight, out_weight):
    unit_rows, normed = normalize(rows_in, ln_gain, ln_bias)
    gate_pre = jnp.dot(normed, gate_weight, preferred_element_type=jnp.float32)
    up_pre = jnp.dot(normed, up_weight, preferred_element_type=jnp.float32)
    squashed = jax.nn.sigmoid(gate_pre)
    silu_val = gate_pre * squashed
    hidden = (silu_val * up_pre).astype(jnp.bfloat16)
    grad_hidden = jnp.dot(grad_rows, out_weight.T, preferred_element_type=jnp.float32)
    grad_gate_pre = (grad_hidden * up_pre * squashed * (1.0 + gate_pre * (1.0 - squashed))).astype(
        jnp.bfloat16
    )
    grad_up_pre = (grad_hidden * silu_val).astype(jnp.bfloat16)
    grad_normed = jnp.dot(
        grad_gate_pre, gate_weight.T, preferred_element_type=jnp.float32
    ) + jnp.dot(grad_up_pre, up_weight.T, preferred_element_type=jnp.float32)
    sum_gain, sum_bias, sum_gate, sum_up, sum_out = totals
    return (
        sum_gain + jnp.sum(grad_normed * unit_rows, axis=0),
        sum_bias + jnp.sum(grad_normed, axis=0),
        sum_gate + inner(normed, grad_gate_pre),
        sum_up + inner(normed, grad_up_pre),
        sum_out + inner(hidden, grad_rows),
    )


def loss_terms(logits, targets, pair_mask):
    bins = logits.shape[-1]
    one_hot = (targets[..., None] == jnp.arange(bins, dtype=jnp.int32)).astype(jnp.float32)
    log_total = jnp.log(jnp.sum(jnp.exp(logits), axis=-1))
    weights_mask = pair_mask.astype(jnp.float32)
    loss_part = jnp.sum(weights_mask * (log_total - jnp.sum(logits * one_hot, axis=-1)))
    soft_probs = jnp.exp(logits - log_total[..., None])
    return (loss_part, soft_probs)


def grad_from(soft_probs, targets, pair_mask, tokens):
    bins = soft_probs.shape[-1]
    one_hot = (targets[..., None] == jnp.arange(bins, dtype=jnp.int32)).astype(jnp.float32)
    weights_mask = pair_mask.astype(jnp.float32)
    return (weights_mask[..., None] * (soft_probs - one_hot) / tokens).astype(jnp.bfloat16)


def shards(
    pair, ln_gain, ln_bias, gate_weight, up_weight, out_weight, head_weight, targets, pair_mask
):
    rows_tile, cols_tile, width = pair.shape
    tokens = cols_tile * lax.axis_size("col")
    block_rows = math.gcd(rows_tile, max(1, 2048 // cols_tile))
    count = rows_tile // block_rows
    blocks = pair.reshape(count, block_rows * cols_tile, width)

    def forward_one(rows_in):
        return advance(rows_in, ln_gain, ln_bias, gate_weight, up_weight, out_weight)

    pair_out = lax.map(forward_one, blocks).reshape(pair.shape)
    rows_pair = lax.all_to_all(pair_out, "col", split_axis=0, concat_axis=1, tiled=True)
    flip_pair = lax.all_to_all(
        jnp.swapaxes(rows_pair, 0, 1), ("row", "col"), split_axis=0, concat_axis=1, tiled=True
    )
    half_rows = jnp.dot(rows_pair, head_weight, preferred_element_type=jnp.float32).astype(
        jnp.bfloat16
    )
    half_flip = jnp.dot(flip_pair, head_weight, preferred_element_type=jnp.float32).astype(
        jnp.bfloat16
    )
    logits = half_rows.astype(jnp.float32) + half_flip.astype(jnp.float32)
    loss_part, soft_probs = loss_terms(logits, targets, pair_mask)
    grad_logits = grad_from(soft_probs, targets, pair_mask, tokens)
    grad_flip = lax.all_to_all(
        jnp.swapaxes(grad_logits, 0, 1), ("row", "col"), split_axis=0, concat_axis=1, tiled=True
    )
    tile_grad, tile_flip = (
        lax.all_to_all(grad_logits, "col", split_axis=1, concat_axis=0, tiled=True),
        lax.all_to_all(grad_flip, "col", split_axis=1, concat_axis=0, tiled=True),
    )
    bins = head_weight.shape[1]
    flat_out = pair_out.reshape(-1, width)
    grad_head = inner(flat_out, tile_grad.reshape(-1, bins)) + inner(
        flat_out, tile_flip.reshape(-1, bins)
    )
    head_back = head_weight.T
    grad_pair = (
        jnp.dot(tile_grad, head_back, preferred_element_type=jnp.float32)
        + jnp.dot(tile_flip, head_back, preferred_element_type=jnp.float32)
    ).astype(jnp.bfloat16)
    grad_blocks = grad_pair.reshape(count, block_rows * cols_tile, width)
    hidden_width = gate_weight.shape[1]
    start = (
        jnp.zeros((width,), jnp.float32),
        jnp.zeros((width,), jnp.float32),
        jnp.zeros((width, hidden_width), jnp.float32),
        jnp.zeros((width, hidden_width), jnp.float32),
        jnp.zeros((hidden_width, width), jnp.float32),
    )

    def backward_one(totals, inputs):
        return (
            retreat(
                totals, inputs[0], inputs[1], ln_gain, ln_bias, gate_weight, up_weight, out_weight
            ),
            None,
        )

    totals, unused = lax.scan(backward_one, start, (blocks, grad_blocks))
    summed = lax.psum(
        (loss_part, totals[0], totals[1], totals[2], totals[3], totals[4], grad_head),
        ("row", "col"),
    )
    loss = summed[0] / (tokens * tokens)
    return (pair_out, loss, summed[1], summed[2], summed[3], summed[4], summed[5], summed[6])


def solution(mesh):
    placed = (
        P("row", "col", None),
        P(),
        P(),
        P(),
        P(),
        P(),
        P(),
        P(("row", "col"), None),
        P(("row", "col"), None),
    )
    return jax.shard_map(
        shards,
        mesh=mesh,
        in_specs=placed,
        out_specs=(P("row", "col", None), P(), P(), P(), P(), P(), P(), P()),
        check_vma=False,
    )
```

profile of v0, /device:TPU:1, one launch (start us, length us, event | category | flops | bytes accessed | tf_op | source)
XLA Modules:
  0.0 416.3 jit_solution(17993143803311774811)
XLA Ops:
  7.2 47.0 %while.29 = (s32[]{:T(128)}, bf16[4,2048,128]{2,1,0:T(8,128)(2,1)}, bf16[4,2048,128]{2,1,0:T(8,128)(2,1)}, f32[128]{0:T(128)}, f32[128]{0:T(128)}, /*index=5*/bf...) while((s32[]{:T(128)}, bf16[4,2048,128]{2,1,0:T(8,128)(2,1)}, ...), condition=%wide.region_3.4_spmd, body=%wide.region_0.3_spmd.sunk | while | flops 817104896 | bytes 21462268 | solution.py:88
  7.2 1.3 convert_reduce_fusion.4
  8.5 1.7 fusion.136
  10.2 4.0 fusion.137
  14.2 4.7 %fusion.138 = bf16[4,2048,128]{2,1,0:T(8,128)(2,1)} fusion(bf16[4,2048,128]{2,1,0:T(8,128)(2,1)} %get-tuple-element.382, s32[]{:T(128)S(6)} %copy.70, bf16[512,128]{1,0:T(8,128)(2,1)S(1)} %copy-done.22, f32[2048,512]{1,0:T(8,128)} %fusion.137, bf16[128,512]{1,0:T(8,128)(2,1)S(1)} %copy-done.12, f32[128]{0:T(128)S(1)} %copy-done.17, ...), kind=kOutput, calls=%fused_computation.4.clone.1 | convolution fusion | flops 545521664 | bytes 6047744 | tf_op jit(solution)/shard_map/while/body/eval_jaxpr/dot_general | solution.py:30
  18.9 1.2 convert_reduce_fusion.4
  20.2 1.7 fusion.136
  22.0 4.0 fusion.137
  26.0 4.7 %fusion.138 = bf16[4,2048,128]{2,1,0:T(8,128)(2,1)} fusion(bf16[4,2048,128]{2,1,0:T(8,128)(2,1)} %get-tuple-element.382, s32[]{:T(128)S(6)} %copy.70, bf16[512,128]{1,0:T(8,128)(2,1)S(1)} %copy-done.22, f32[2048,512]{1,0:T(8,128)} %fusion.137, bf16[128,512]{1,0:T(8,128)(2,1)S(1)} %copy-done.12, f32[128]{0:T(128)S(1)} %copy-done.17, ...), kind=kOutput, calls=%fused_computation.4.clone.1 | convolution fusion | flops 545521664 | bytes 6047744 | tf_op jit(solution)/shard_map/while/body/eval_jaxpr/dot_general | solution.py:30
  30.7 1.2 convert_reduce_fusion.4
  31.9 1.7 fusion.136
  33.7 4.0 fusion.137
  37.7 4.7 %fusion.138 = bf16[4,2048,128]{2,1,0:T(8,128)(2,1)} fusion(bf16[4,2048,128]{2,1,0:T(8,128)(2,1)} %get-tuple-element.382, s32[]{:T(128)S(6)} %copy.70, bf16[512,128]{1,0:T(8,128)(2,1)S(1)} %copy-done.22, f32[2048,512]{1,0:T(8,128)} %fusion.137, bf16[128,512]{1,0:T(8,128)(2,1)S(1)} %copy-done.12, f32[128]{0:T(128)S(1)} %copy-done.17, ...), kind=kOutput, calls=%fused_computation.4.clone.1 | convolution fusion | flops 545521664 | bytes 6047744 | tf_op jit(solution)/shard_map/while/body/eval_jaxpr/dot_general | solution.py:30
  42.4 1.2 convert_reduce_fusion.4
  43.7 1.7 fusion.136
  45.4 4.0 fusion.137
  49.4 4.7 %fusion.138 = bf16[4,2048,128]{2,1,0:T(8,128)(2,1)} fusion(bf16[4,2048,128]{2,1,0:T(8,128)(2,1)} %get-tuple-element.382, s32[]{:T(128)S(6)} %copy.70, bf16[512,128]{1,0:T(8,128)(2,1)S(1)} %copy-done.22, f32[2048,512]{1,0:T(8,128)} %fusion.137, bf16[128,512]{1,0:T(8,128)(2,1)S(1)} %copy-done.12, f32[128]{0:T(128)S(1)} %copy-done.17, ...), kind=kOutput, calls=%fused_computation.4.clone.1 | convolution fusion | flops 545521664 | bytes 6047744 | tf_op jit(solution)/shard_map/while/body/eval_jaxpr/dot_general | solution.py:30
  54.2 34.8 %all_to_all.90 = bf16[64,128,128]{2,1,0:T(8,128)(2,1)S(1)} all-to-all(bf16[64,128,128]{2,1,0:T(8,128)(2,1)} %bitcast.213), channel_id=1, replica_groups=mesh['row'=16,'col'=8] {'col'}, dimensions={0} | all-to-all | bytes 4194304 | tf_op jit(solution)/shard_map/all_to_all | solution.py:89
  89.1 2.7 copy.30
  91.8 8.6 %all-to-all-start.1 = ((bf16[1024,8,128]{2,1,0:T(8,128)(2,1)}), bf16[1024,8,128]{2,1,0:T(8,128)(2,1)}, u32[]{:S(2)}, u32[]{:S(2)}) async-start(bf16[1024,8,128]{2,1,0:T(8,128)(2,1)} %copy.30), calls=%async_computation.1 | async-start | bytes 4194304 | tf_op jit(solution)/shard_map/all_to_all | solution.py:90
  101.2 27.3 %all-to-all-done.1 = bf16[1024,8,128]{2,1,0:T(8,128)(2,1)} async-done(((bf16[1024,8,128]{2,1,0:T(8,128)(2,1)}), bf16[1024,8,128]{2,1,0:T(8,128)(2,1)}, u32[]{:S(2)}, u32[]{:S(2)}) %all-to-all-start.1) | async-done | bytes 2097184 | tf_op jit(solution)/shard_map/all_to_all | solution.py:90
  128.5 2.8 exponential_reduce_fusion
  132.2 1.9 fusion.68
  134.1 2.6 copy.35
  136.7 2.3 reshape.76
  139.1 6.3 %all-to-all-start.3 = ((bf16[128,2,2048]{2,1,0:T(2,128)(2,1)}), bf16[128,2,2048]{2,1,0:T(2,128)(2,1)}, u32[]{:S(2)}, u32[]{:S(2)}) async-start(bf16[128,2,2048]{2,1,0:T(2,128)(2,1)} %reshape.76), calls=%async_computation.3 | async-start | bytes 2097152 | tf_op jit(solution)/shard_map/all_to_all | solution.py:102
  146.2 1.7 copy.32
  147.9 2.7 reshape.74
  150.6 12.1 %all-to-all-done.3 = bf16[128,2,2048]{2,1,0:T(2,128)(2,1)} async-done(((bf16[128,2,2048]{2,1,0:T(2,128)(2,1)}), bf16[128,2,2048]{2,1,0:T(2,128)(2,1)}, u32[]{:S(2)}, u32[]{:S(2)}) %all-to-all-start.3) | async-done | bytes 1048608 | tf_op jit(solution)/shard_map/all_to_all | solution.py:102
  162.7 4.6 %all-to-all-start.2 = ((bf16[8,2,32768]{2,1,0:T(2,128)(2,1)}), bf16[8,2,32768]{2,1,0:T(2,128)(2,1)S(1)}, u32[]{:S(2)}, u32[]{:S(2)}) async-start(bf16[8,2,32768]{2,1,0:T(2,128)(2,1)} %reshape.74), calls=%async_computation.2 | async-start | bytes 2097152 | tf_op jit(solution)/shard_map/all_to_all | solution.py:106
  167.3 3.8 reshape.77
  171.5 1.4 copy.66
  172.8 2.7 reshape.78
  175.5 7.5 %all-to-all-done.2 = bf16[8,2,32768]{2,1,0:T(2,128)(2,1)S(1)} async-done(((bf16[8,2,32768]{2,1,0:T(2,128)(2,1)}), bf16[8,2,32768]{2,1,0:T(2,128)(2,1)S(1)}, u32[]{:S(2)}, u32[]{:S(2)}) %all-to-all-start.2) | async-done | bytes 1048608 | tf_op jit(solution)/shard_map/all_to_all | solution.py:106
  183.0 4.2 %all-to-all-start.4 = ((bf16[8,2,32768]{2,1,0:T(2,128)(2,1)}), bf16[8,2,32768]{2,1,0:T(2,128)(2,1)}, u32[]{:S(2)}, u32[]{:S(2)}) async-start(bf16[8,2,32768]{2,1,0:T(2,128)(2,1)} %reshape.78), calls=%async_computation.4 | async-start | bytes 2097152 | tf_op jit(solution)/shard_map/all_to_all | solution.py:107
  187.4 3.1 reshape.75
  190.5 3.1 copy.33
  193.6 1.9 copy.34
  195.5 3.9 fusion.79
  199.4 3.5 all-to-all-done.4
  203.0 3.1 reshape.79
  206.1 1.9 copy.39
  208.0 4.8 %add_convert_fusion = bf16[64,128,128]{2,1,0:T(8,128)(2,1)} fusion(f32[64,128,128]{2,1,0:T(8,128)} %fusion.79, bf16[64,128,64]{1,2,0:T(8,128)(2,1)} %bitcast.225, bf16[128,64]{0,1:T(8,128)(2,1)S(1)} %copy-done), kind=kOutput, calls=%fused_computation.67 | convolution fusion | flops 136314880 | bytes 7356416 | tf_op jit(solution)/shard_map/dot_general | solution.py:117
  212.9 43.0 %while.30 = (s32[]{:T(128)}, f32[128]{0:T(128)S(1)}, f32[128]{0:T(128)S(1)}, f32[128,512]{1,0:T(8,128)S(1)}, f32[128,512]{1,0:T(8,128)S(1)}, /*index=5*/f32[512,...) while((s32[]{:T(128)}, f32[128]{0:T(128)S(1)}, ...), condition=%wide.region_13.14_spmd.clone, body=%wide.region_8.13_spmd.clone.sunk | while | flops 2177501440 | bytes 55328988 | solution.py:137
  216.1 1.3 fusion.159
  217.5 2.1 multiply_convert_fusion.11
  219.6 1.1 convolution_add_fusion.7
  226.8 1.3 fusion.159
  228.2 2.1 multiply_convert_fusion.11
  230.3 1.1 convolution_add_fusion.7
  237.5 1.3 fusion.159
  238.9 2.1 multiply_convert_fusion.11
  241.0 1.1 convolution_add_fusion.7
  248.2 1.3 fusion.159
  249.6 2.1 multiply_convert_fusion.11
  251.7 1.1 convolution_add_fusion.7
  256.8 2.7 fusion.75
  259.6 3.1 copy.40
  262.7 2.8 convolution_add_fusion.4
  265.5 64.7 %all-reduce = (f32[]{:T(128)}, f32[128]{0:T(128)}, f32[128]{0:T(128)}, f32[128,64]{0,1:T(8,128)}) all-reduce(f32[]{:T(128)} %get-tuple-element.229, f32[128]{0:T(128)S(1)} %get-tuple-element.122, f32[128]{0:T(128)S(1)} %get-tuple-element.123, f32[128,64]{0,1:T(8,128)S(1)} %convolution_add_fusion.4), channel_id=1, replica_groups=mesh['row'=16,'col'=8] {'row','col'}, use_global_device_ids=true, to_apply=%region_7.8 | all-reduce | flops 8449 | bytes 67592 | tf_op jit(solution)/shard_map/psum | solution.py:138
  330.8 72.6 %all-reduce.4.cloned.1.call-done = (f32[128,512]{1,0:T(8,128)}, f32[128,512]{1,0:T(8,128)}, f32[512,128]{1,0:T(8,128)}) async-done(((f32[128,512]{1,0:T(8,128)}, f32[128,512]{1,0:T(8,128)}, f32[512,128]{1,0:T(8,128)}), (f32[128,512]{1,0:T(8,128)}, f32[128,512]{1,0:T(8,128)}, f32[512,128]{1,0:T(8,128)})) %all-reduce.4.cloned.1.call-update) | async-done | bytes 786448 | tf_op jit(solution)/shard_map/psum | solution.py:138
  403.3 1.7 copy.95
  405.0 1.7 copy.96
  406.7 1.7 copy.97
  (146 shorter events, 28.3 us)
Async XLA Ops:
  7.2 93.2 %copy-start = (bf16[128,64]{0,1:T(8,128)(2,1)S(1)}, bf16[128,64]{0,1:T(8,128)(2,1)}, u32[]{:S(2)}) copy-start(bf16[128,64]{0,1:T(8,128)(2,1)} %param.19) | copy-start | bytes 49156
  10.2 4.0 copy-start.2
  10.2 4.0 copy-start.12
  10.2 4.0 copy-start.15
  10.2 4.0 copy-start.17
  10.2 4.0 copy-start.22
  21.9 4.0 copy-start.2
  21.9 4.0 copy-start.12
  21.9 4.0 copy-start.15
  21.9 4.0 copy-start.17
  22.0 4.0 copy-start.22
  33.6 4.0 copy-start.2
  33.7 4.0 copy-start.12
  33.7 4.0 copy-start.15
  33.7 4.0 copy-start.17
  33.7 4.0 copy-start.22
  45.4 4.0 copy-start.2
  45.4 4.0 copy-start.12
  45.4 4.0 copy-start.15
  45.4 4.0 copy-start.17
  45.4 4.0 copy-start.22
  91.8 8.6 %copy-start.21 = (s32[8,1024]{1,0:T(8,128)S(1)}, s32[8,1024]{1,0:T(8,128)}, u32[]{:S(2)}) copy-start(s32[8,1024]{1,0:T(8,128)} %param.21) | copy-start | bytes 98308
  91.8 36.7 %all-to-all-start.1 = ((bf16[1024,8,128]{2,1,0:T(8,128)(2,1)}), bf16[1024,8,128]{2,1,0:T(8,128)(2,1)}, u32[]{:S(2)}, u32[]{:S(2)}) async-start(bf16[1024,8,128]{2,1,0:T(8,128)(2,1)} %copy.30), calls=%async_computation.1 | async-start | bytes 4194304 | tf_op jit(solution)/shard_map/all_to_all | solution.py:90
  100.4 28.1 %copy-start.20 = (s32[8,1024]{1,0:T(8,128)S(1)}, s32[8,1024]{1,0:T(8,128)}, u32[]{:S(2)}) copy-start(s32[8,1024]{1,0:T(8,128)} %param.20) | copy-start | bytes 98308
  131.3 1.0 copy-start.9
  139.0 6.3 %copy-start.10 = (bf16[8,1024,64]{1,2,0:T(8,128)(2,1)S(1)}, bf16[8,1024,64]{1,2,0:T(8,128)(2,1)}, u32[]{:S(2)}) copy-start(bf16[8,1024,64]{1,2,0:T(8,128)(2,1)} %copy-done.9) | copy-start | bytes 3145732
  139.1 23.7 %all-to-all-start.3 = ((bf16[128,2,2048]{2,1,0:T(2,128)(2,1)}), bf16[128,2,2048]{2,1,0:T(2,128)(2,1)}, u32[]{:S(2)}, u32[]{:S(2)}) async-start(bf16[128,2,2048]{2,1,0:T(2,128)(2,1)} %reshape.76), calls=%async_computation.3 | async-start | bytes 2097152 | tf_op jit(solution)/shard_map/all_to_all | solution.py:102
  162.7 20.3 %all-to-all-start.2 = ((bf16[8,2,32768]{2,1,0:T(2,128)(2,1)}), bf16[8,2,32768]{2,1,0:T(2,128)(2,1)S(1)}, u32[]{:S(2)}, u32[]{:S(2)}) async-start(bf16[8,2,32768]{2,1,0:T(2,128)(2,1)} %reshape.74), calls=%async_computation.2 | async-start | bytes 2097152 | tf_op jit(solution)/shard_map/all_to_all | solution.py:106
  183.0 4.3 %copy-start.11 = (bf16[8,2,32768]{2,1,0:T(2,128)(2,1)}, bf16[8,2,32768]{2,1,0:T(2,128)(2,1)S(1)}, u32[]{:S(2)}) copy-start(bf16[8,2,32768]{2,1,0:T(2,128)(2,1)S(1)} %all-to-all-done.2) | copy-start | bytes 3145732
  183.0 19.9 %all-to-all-start.4 = ((bf16[8,2,32768]{2,1,0:T(2,128)(2,1)}), bf16[8,2,32768]{2,1,0:T(2,128)(2,1)}, u32[]{:S(2)}, u32[]{:S(2)}) async-start(bf16[8,2,32768]{2,1,0:T(2,128)(2,1)} %reshape.78), calls=%async_computation.4 | async-start | bytes 2097152 | tf_op jit(solution)/shard_map/all_to_all | solution.py:107
  187.3 216.1 %all-reduce.4.cloned.1.call-start = ((), (), s32[]{:S(2)}) async-start(), calls=%async_computation.5 | async-start | bytes 1572864 | tf_op jit(solution)/shard_map/psum | solution.py:138
  206.1 1.9 copy-start.5
  208.0 4.8 %copy-start.3 = (bf16[4,2048,128]{2,1,0:T(8,128)(2,1)S(1)}, bf16[4,2048,128]{2,1,0:T(8,128)(2,1)}, u32[]{:S(2)}) copy-start(bf16[4,2048,128]{2,1,0:T(8,128)(2,1)} %get-tuple-element.458) | copy-start | bytes 6291460
  208.0 4.8 %copy-start.4 = (bf16[128,512]{1,0:T(8,128)(2,1)S(1)}, bf16[128,512]{1,0:T(8,128)(2,1)}, u32[]{:S(2)}) copy-start(bf16[128,512]{1,0:T(8,128)(2,1)} %get-tuple-element.459) | copy-start | bytes 393220
  208.0 4.8 %copy-start.13 = (bf16[128,512]{1,0:T(8,128)(2,1)S(1)}, bf16[128,512]{1,0:T(8,128)(2,1)}, u32[]{:S(2)}) copy-start(bf16[128,512]{1,0:T(8,128)(2,1)} %get-tuple-element.472) | copy-start | bytes 393220
  208.0 4.8 %copy-start.16 = (f32[128]{0:T(128)S(1)}, f32[128]{0:T(128)}, u32[]{:S(2)}) copy-start(f32[128]{0:T(128)} %get-tuple-element.473) | copy-start | bytes 1540
  208.0 4.8 %copy-start.18 = (f32[128]{0:T(128)S(1)}, f32[128]{0:T(128)}, u32[]{:S(2)}) copy-start(f32[128]{0:T(128)} %get-tuple-element.474) | copy-start | bytes 1540
  208.0 4.8 %copy-start.23 = (bf16[512,128]{1,0:T(8,128)(2,1)S(1)}, bf16[512,128]{1,0:T(8,128)(2,1)}, u32[]{:S(2)}) copy-start(bf16[512,128]{1,0:T(8,128)(2,1)} %get-tuple-element.480) | copy-start | bytes 393220
  214.5 1.6 copy-start.14
  225.2 1.6 copy-start.14
  235.9 1.6 copy-start.14
  246.6 1.6 copy-start.14
  255.9 0.7 copy-start.7
  255.9 0.8 copy-start.8
  255.9 0.9 copy-start.19
  255.9 3.6 copy-start.6
  262.7 145.7 %copy-start.1 = (bf16[128,64]{0,1:T(8,128)(2,1)S(1)}, bf16[128,64]{0,1:T(8,128)(2,1)}, u32[]{:S(2)}) copy-start(bf16[128,64]{0,1:T(8,128)(2,1)} %param.19) | copy-start | bytes 49156
Sparse Core Ops, SparseCore 0:
  256.9 146.3 all-reduce.3
where the time goes:
time: 418 us; the launch traced here: 416 us
  waiting for transfers between devices  123 us (29%)
  blocking collectives  99.5 us (24%)
  matrix products  88.2 us (21%)
  local copies, waits for them, and re-layouts  46 us (11%)
  starting transfers between devices  23.7 us (6%)
  other arithmetic  18.7 us (4%)
  between operations  16.2 us (4%)
    psum x1, waiting for transfers between devices, shards(): lax.psum((loss_part, totals[0], totals[1], totals[2], totals[3], totals[4...  72.6 us
    psum x1, blocking collectives, shards(): lax.psum((loss_part, totals[0], totals[1], totals[2], totals[3], totals[4...  64.7 us
    all_to_all x1, blocking collectives, shards(): lax.all_to_all(pair_out, 'col', split_axis=0, concat_axis=1, tiled=True)  34.8 us
    all_to_all x1, waiting for transfers between devices, shards(): lax.all_to_all(jnp.swapaxes(rows_pair, 0, 1), ('row', 'col'), split_axis=...  27.3 us
    unnamed x45, local copies, waits for them, and re-layouts  23.8 us
    dot_general x14, matrix products, inner(): lax.dot_general(left, right, (((0,), (0,)), ((), ())), preferred_element_...  19.9 us
    dot_general x4, matrix products, advance(): update = jnp.dot(hidden, out_weight, preferred_element_type=jnp.float32)  18.9 us
    dot_general x4, matrix products, advance(): gate_pre = jnp.dot(normed, gate_weight, preferred_element_type=jnp.float32)  15.9 us
  transfers between devices with their start and end apart: 5, of which 5 were waited for; matrix products, arithmetic and copies ran while one was open for 8% of the time, Pallas kernels for 0%

commit v1 on v0

--- a/solution.py
+++ b/solution.py
@@ -136,8 +136,10 @@
 
     totals, unused = lax.scan(backward_one, start, (blocks, grad_blocks))
     summed = lax.psum(
-        (loss_part, totals[0], totals[1], totals[2], totals[3], totals[4], grad_head),
-        ("row", "col"),
+        lax.psum(
+            (loss_part, totals[0], totals[1], totals[2], totals[3], totals[4], grad_head), "col"
+        ),
+        "row",
     )
     loss = summed[0] / (tokens * tokens)
     return (pair_out, loss, summed[1], summed[2], summed[3], summed[4], summed[5], summed[6])

time: 418 us -> 477 us (1.14)
  blocking collectives: 99.5 us -> 130 us
  waiting for transfers between devices: 123 us -> 151 us
    psum x0 -> x1, blocking collectives: none -> 62.4 us  [shards(): lax.psum(lax.psum((loss_part, totals[0], totals[1], totals[2], totals[3],...]
    psum x1, blocking collectives: 64.7 us -> 32.5 us  [shards(): lax.psum((loss_part, totals[0], totals[1], totals[2], totals[3], totals[4...]
    psum x0 -> x1, waiting for transfers between devices: none -> 19.1 us  [shards(): lax.psum(lax.psum((loss_part, totals[0], totals[1], totals[2], totals[3],...]
    psum x1, waiting for transfers between devices: 72.6 us -> 80 us  [shards(): lax.psum((loss_part, totals[0], totals[1], totals[2], totals[3], totals[4...]
    unnamed x45 -> x47, local copies, waits for them, and re-layouts: 23.8 us -> 23.8 us
  transfers between devices with their start and end apart: 5 -> 6, of which waited for: 5 -> 6; matrix products, arithmetic and copies ran while one was open for 8% -> 8% of each run, Pallas kernels for 0% -> 0%
where the time goes in v1:
time: 477 us; the launch traced here: 475 us
  waiting for transfers between devices  151 us (32%)
  blocking collectives  130 us (27%)
  matrix products  87.7 us (18%)
  local copies, waits for them, and re-layouts  46.7 us (10%)
  starting transfers between devices  24 us (5%)
  other arithmetic  19.7 us (4%)
  between operations  16.2 us (3%)
    psum x1, waiting for transfers between devices, shards(): lax.psum((loss_part, totals[0], totals[1], totals[2], totals[3], totals[4...  80 us
    psum x1, blocking collectives, shards(): lax.psum(lax.psum((loss_part, totals[0], totals[1], totals[2], totals[3],...  62.4 us
    all_to_all x1, blocking collectives, shards(): lax.all_to_all(pair_out, 'col', split_axis=0, concat_axis=1, tiled=True)  34.8 us
    psum x1, blocking collectives, shards(): lax.psum((loss_part, totals[0], totals[1], totals[2], totals[3], totals[4...  32.5 us
    all_to_all x1, waiting for transfers between devices, shards(): lax.all_to_all(jnp.swapaxes(rows_pair, 0, 1), ('row', 'col'), split_axis=...  27.3 us
    unnamed x47, local copies, waits for them, and re-layouts  23.8 us
    dot_general x14, matrix products, inner(): lax.dot_general(left, right, (((0,), (0,)), ((), ())), preferred_element_...  19.3 us
    psum x1, waiting for transfers between devices, shards(): lax.psum(lax.psum((loss_part, totals[0], totals[1], totals[2], totals[3],...  19.1 us
  transfers between devices with their start and end apart: 6, of which 6 were waited for; matrix products, arithmetic and copies ran while one was open for 8% of the time, Pallas kernels for 0%

profile of v1, /device:TPU:1, one launch (start us, length us, event | category | flops | bytes accessed | tf_op | source)
XLA Modules:
  0.0 475.4 jit_solution(1439036759768985952)
XLA Ops:
  7.2 47.0 %while.29 = (s32[]{:T(128)}, bf16[4,2048,128]{2,1,0:T(8,128)(2,1)}, bf16[4,2048,128]{2,1,0:T(8,128)(2,1)}, f32[128]{0:T(128)}, f32[128]{0:T(128)}, /*index=5*/bf...) while((s32[]{:T(128)}, bf16[4,2048,128]{2,1,0:T(8,128)(2,1)}, ...), condition=%wide.region_3.4_spmd, body=%wide.region_0.3_spmd.sunk | while | flops 817104896 | bytes 21462268 | solution.py:88
  7.2 1.3 convert_reduce_fusion.4
  8.5 1.7 fusion.136
  10.2 4.0 fusion.137
  14.2 4.7 fusion.138
  18.9 1.2 convert_reduce_fusion.4
  20.2 1.7 fusion.136
  22.0 4.0 fusion.137
  26.0 4.7 fusion.138
  30.7 1.2 convert_reduce_fusion.4
  32.0 1.7 fusion.136
  33.7 4.0 fusion.137
  37.7 4.7 fusion.138
  42.4 1.2 convert_reduce_fusion.4
  43.7 1.7 fusion.136
  45.5 4.0 fusion.137
  49.5 4.7 fusion.138
  54.2 34.8 %all_to_all.90 = bf16[64,128,128]{2,1,0:T(8,128)(2,1)S(1)} all-to-all(bf16[64,128,128]{2,1,0:T(8,128)(2,1)} %bitcast.213), channel_id=1, replica_groups=mesh['row'=16,'col'=8] {'col'}, dimensions={0} | all-to-all | bytes 4194304 | tf_op jit(solution)/shard_map/all_to_all | solution.py:89
  89.1 2.7 copy.30
  91.8 8.6 %all-to-all-start.1 = ((bf16[1024,8,128]{2,1,0:T(8,128)(2,1)}), bf16[1024,8,128]{2,1,0:T(8,128)(2,1)}, u32[]{:S(2)}, u32[]{:S(2)}) async-start(bf16[1024,8,128]{2,1,0:T(8,128)(2,1)} %copy.30), calls=%async_computation.1 | async-start | bytes 4194304 | tf_op jit(solution)/shard_map/all_to_all | solution.py:90
  101.3 27.3 %all-to-all-done.1 = bf16[1024,8,128]{2,1,0:T(8,128)(2,1)} async-done(((bf16[1024,8,128]{2,1,0:T(8,128)(2,1)}), bf16[1024,8,128]{2,1,0:T(8,128)(2,1)}, u32[]{:S(2)}, u32[]{:S(2)}) %all-to-all-start.1) | async-done | bytes 2097184 | tf_op jit(solution)/shard_map/all_to_all | solution.py:90
  128.6 2.8 exponential_reduce_fusion
  132.3 1.9 fusion.68
  134.1 2.6 copy.35
  136.8 2.3 reshape.76
  139.1 6.3 %all-to-all-start.3 = ((bf16[128,2,2048]{2,1,0:T(2,128)(2,1)}), bf16[128,2,2048]{2,1,0:T(2,128)(2,1)}, u32[]{:S(2)}, u32[]{:S(2)}) async-start(bf16[128,2,2048]{2,1,0:T(2,128)(2,1)} %reshape.76), calls=%async_computation.3 | async-start | bytes 2097152 | tf_op jit(solution)/shard_map/all_to_all | solution.py:102
  145.4 1.8 multiply_convert_fusion.7
  147.2 2.6 copy.32
  149.9 2.7 reshape.74
  152.5 10.2 %all-to-all-done.3 = bf16[128,2,2048]{2,1,0:T(2,128)(2,1)} async-done(((bf16[128,2,2048]{2,1,0:T(2,128)(2,1)}), bf16[128,2,2048]{2,1,0:T(2,128)(2,1)}, u32[]{:S(2)}, u32[]{:S(2)}) %all-to-all-start.3) | async-done | bytes 1048608 | tf_op jit(solution)/shard_map/all_to_all | solution.py:102
  162.8 4.6 all-to-all-start.2
  167.3 3.8 reshape.77
  171.5 1.4 copy.66
  172.9 2.7 reshape.78
  175.5 7.5 %all-to-all-done.2 = bf16[8,2,32768]{2,1,0:T(2,128)(2,1)S(1)} async-done(((bf16[8,2,32768]{2,1,0:T(2,128)(2,1)}), bf16[8,2,32768]{2,1,0:T(2,128)(2,1)S(1)}, u32[]{:S(2)}, u32[]{:S(2)}) %all-to-all-start.2) | async-done | bytes 1048608 | tf_op jit(solution)/shard_map/all_to_all | solution.py:106
  183.1 4.2 all-to-all-start.4
  187.4 3.1 reshape.75
  190.5 1.9 copy.34
  192.5 3.9 fusion.79
  196.4 6.6 %all-to-all-done.4 = bf16[8,2,32768]{2,1,0:T(2,128)(2,1)} async-done(((bf16[8,2,32768]{2,1,0:T(2,128)(2,1)}), bf16[8,2,32768]{2,1,0:T(2,128)(2,1)}, u32[]{:S(2)}, u32[]{:S(2)}) %all-to-all-start.4) | async-done | bytes 1048608 | tf_op jit(solution)/shard_map/all_to_all | solution.py:107
  203.0 3.1 reshape.79
  206.1 1.9 copy.39
  208.1 4.8 %add_convert_fusion = bf16[64,128,128]{2,1,0:T(8,128)(2,1)} fusion(f32[64,128,128]{2,1,0:T(8,128)} %fusion.79, bf16[64,128,64]{1,2,0:T(8,128)(2,1)} %bitcast.223, bf16[128,64]{0,1:T(8,128)(2,1)S(1)} %copy-done), kind=kOutput, calls=%fused_computation.67 | convolution fusion | flops 136314880 | bytes 7356416 | tf_op jit(solution)/shard_map/dot_general | solution.py:117
  212.9 42.8 %while.30 = (s32[]{:T(128)}, f32[128]{0:T(128)S(1)}, f32[128]{0:T(128)S(1)}, f32[128,512]{1,0:T(8,128)S(1)}, f32[128,512]{1,0:T(8,128)S(1)}, /*index=5*/f32[512,...) while((s32[]{:T(128)}, f32[128]{0:T(128)S(1)}, ...), condition=%wide.region_14.15_spmd.clone, body=%wide.region_9.14_spmd.clone.sunk | while | flops 2177501440 | bytes 55328988 | solution.py:137
  216.2 1.3 fusion.159
  217.5 2.1 multiply_convert_fusion.11
  226.9 1.3 fusion.159
  228.2 2.1 multiply_convert_fusion.11
  230.4 1.1 convolution_add_fusion.7
  237.6 1.3 fusion.159
  238.9 2.1 multiply_convert_fusion.11
  248.3 1.3 fusion.159
  249.6 2.1 multiply_convert_fusion.11
  256.9 80.0 %all-reduce.9.cloned.1.call-done = (f32[128,512]{1,0:T(8,128)}, f32[128,512]{1,0:T(8,128)}, f32[512,128]{1,0:T(8,128)}) async-done(((f32[128,512]{1,0:T(8,128)}, f32[128,512]{1,0:T(8,128)}, f32[512,128]{1,0:T(8,128)}), (f32[128,512]{1,0:T(8,128)}, f32[128,512]{1,0:T(8,128)}, f32[512,128]{1,0:T(8,128)})) %all-reduce.9.cloned.1.call-update) | async-done | bytes 786448 | tf_op jit(solution)/shard_map/psum | solution.py:139
  336.9 3.5 copy.33
  340.5 2.5 fusion.75
  343.0 2.4 copy.40
  345.4 2.4 convolution_add_fusion.4
  347.8 32.5 %all-reduce.2 = (f32[]{:T(128)}, f32[128]{0:T(128)S(1)}, f32[128]{0:T(128)S(1)}, f32[128,64]{0,1:T(8,128)S(1)}) all-reduce(f32[]{:T(128)} %get-tuple-element.236, f32[128]{0:T(128)S(1)} %get-tuple-element.122, f32[128]{0:T(128)S(1)} %get-tuple-element.123, ...), channel_id=1, replica_groups=mesh['row'=16,'col'=8] {'col'}, use_global_device_ids=true, to_apply=%region_7.8 | all-reduce | flops 8449 | bytes 67592 | tf_op jit(solution)/shard_map/psum | solution.py:139
  380.3 62.4 %all-reduce = (f32[]{:T(128)}, f32[128]{0:T(128)}, f32[128]{0:T(128)}, f32[128,64]{0,1:T(8,128)}) all-reduce(f32[]{:T(128)} %get-tuple-element.222, f32[128]{0:T(128)S(1)} %get-tuple-element.223, f32[128]{0:T(128)S(1)} %get-tuple-element.224, f32[128,64]{0,1:T(8,128)S(1)} %get-tuple-element.225), channel_id=1, replica_groups=mesh['row'=16,'col'=8] {'row'}, use_global_device_ids=true, to_apply=%region_8.9 | all-reduce | flops 8449 | bytes 67592 | tf_op jit(solution)/shard_map/psum | solution.py:138
  443.3 19.1 %all-reduce.7.cloned.1.call-done = (f32[128,512]{1,0:T(8,128)}, f32[128,512]{1,0:T(8,128)}, f32[512,128]{1,0:T(8,128)}) async-done(((f32[128,512]{1,0:T(8,128)}, f32[128,512]{1,0:T(8,128)}, f32[512,128]{1,0:T(8,128)}), (f32[128,512]{1,0:T(8,128)}, f32[128,512]{1,0:T(8,128)}, f32[512,128]{1,0:T(8,128)})) %all-reduce.7.cloned.1.call-update) | async-done | bytes 786448 | tf_op jit(solution)/shard_map/psum | solution.py:138
  462.5 1.7 copy.98
  464.1 1.7 copy.99
  465.8 1.7 copy.100
  (152 shorter events, 31.1 us)
Async XLA Ops:
  7.2 93.3 %copy-start = (bf16[128,64]{0,1:T(8,128)(2,1)S(1)}, bf16[128,64]{0,1:T(8,128)(2,1)}, u32[]{:S(2)}) copy-start(bf16[128,64]{0,1:T(8,128)(2,1)} %param.19) | copy-start | bytes 49156
  10.2 4.0 copy-start.2
  10.2 4.0 copy-start.13
  10.2 4.0 copy-start.16
  10.2 4.0 copy-start.18
  10.2 4.0 copy-start.23
  21.9 4.0 copy-start.2
  21.9 4.0 copy-start.13
  21.9 4.0 copy-start.16
  21.9 4.0 copy-start.18
  22.0 4.0 copy-start.23
  33.7 4.0 copy-start.2
  33.7 4.0 copy-start.13
  33.7 4.0 copy-start.16
  33.7 4.0 copy-start.18
  33.7 4.0 copy-start.23
  45.4 4.0 copy-start.2
  45.4 4.0 copy-start.13
  45.4 4.0 copy-start.16
  45.4 4.0 copy-start.18
  45.4 4.0 copy-start.23
  91.8 8.6 %copy-start.22 = (s32[8,1024]{1,0:T(8,128)S(1)}, s32[8,1024]{1,0:T(8,128)}, u32[]{:S(2)}) copy-start(s32[8,1024]{1,0:T(8,128)} %param.21) | copy-start | bytes 98308
  91.8 36.7 %all-to-all-start.1 = ((bf16[1024,8,128]{2,1,0:T(8,128)(2,1)}), bf16[1024,8,128]{2,1,0:T(8,128)(2,1)}, u32[]{:S(2)}, u32[]{:S(2)}) async-start(bf16[1024,8,128]{2,1,0:T(8,128)(2,1)} %copy.30), calls=%async_computation.1 | async-start | bytes 4194304 | tf_op jit(solution)/shard_map/all_to_all | solution.py:90
  100.4 28.1 %copy-start.21 = (s32[8,1024]{1,0:T(8,128)S(1)}, s32[8,1024]{1,0:T(8,128)}, u32[]{:S(2)}) copy-start(s32[8,1024]{1,0:T(8,128)} %param.20) | copy-start | bytes 98308
  131.3 1.0 copy-start.10
  139.1 6.3 %copy-start.11 = (bf16[8,1024,64]{1,2,0:T(8,128)(2,1)S(1)}, bf16[8,1024,64]{1,2,0:T(8,128)(2,1)}, u32[]{:S(2)}) copy-start(bf16[8,1024,64]{1,2,0:T(8,128)(2,1)} %copy-done.10) | copy-start | bytes 3145732
  139.1 23.7 %all-to-all-start.3 = ((bf16[128,2,2048]{2,1,0:T(2,128)(2,1)}), bf16[128,2,2048]{2,1,0:T(2,128)(2,1)}, u32[]{:S(2)}, u32[]{:S(2)}) async-start(bf16[128,2,2048]{2,1,0:T(2,128)(2,1)} %reshape.76), calls=%async_computation.3 | async-start | bytes 2097152 | tf_op jit(solution)/shard_map/all_to_all | solution.py:102
  162.8 20.3 %all-to-all-start.2 = ((bf16[8,2,32768]{2,1,0:T(2,128)(2,1)}), bf16[8,2,32768]{2,1,0:T(2,128)(2,1)S(1)}, u32[]{:S(2)}, u32[]{:S(2)}) async-start(bf16[8,2,32768]{2,1,0:T(2,128)(2,1)} %reshape.74), calls=%async_computation.2 | async-start | bytes 2097152 | tf_op jit(solution)/shard_map/all_to_all | solution.py:106
  183.1 4.3 copy-start.12
  183.1 19.9 %all-to-all-start.4 = ((bf16[8,2,32768]{2,1,0:T(2,128)(2,1)}), bf16[8,2,32768]{2,1,0:T(2,128)(2,1)}, u32[]{:S(2)}, u32[]{:S(2)}) async-start(bf16[8,2,32768]{2,1,0:T(2,128)(2,1)} %reshape.78), calls=%async_computation.4 | async-start | bytes 2097152 | tf_op jit(solution)/shard_map/all_to_all | solution.py:107
  187.3 149.6 %all-reduce.9.cloned.1.call-start = ((), (), s32[]{:S(2)}) async-start(), calls=%async_computation.6 | async-start | bytes 1572864 | tf_op jit(solution)/shard_map/psum | solution.py:139
  190.5 5.9 %copy-start.5 = (bf16[1024,8,64]{2,1,0:T(8,128)(2,1)}, bf16[1024,8,64]{2,1,0:T(8,128)(2,1)S(1)}, u32[]{:S(2)}) copy-start(bf16[1024,8,64]{2,1,0:T(8,128)(2,1)S(1)} %reshape.75) | copy-start | bytes 3145732
  206.1 1.9 copy-start.6
  208.0 4.9 %copy-start.3 = (bf16[4,2048,128]{2,1,0:T(8,128)(2,1)S(1)}, bf16[4,2048,128]{2,1,0:T(8,128)(2,1)}, u32[]{:S(2)}) copy-start(bf16[4,2048,128]{2,1,0:T(8,128)(2,1)} %get-tuple-element.471) | copy-start | bytes 6291460
  208.0 4.9 %copy-start.4 = (bf16[128,512]{1,0:T(8,128)(2,1)S(1)}, bf16[128,512]{1,0:T(8,128)(2,1)}, u32[]{:S(2)}) copy-start(bf16[128,512]{1,0:T(8,128)(2,1)} %get-tuple-element.472) | copy-start | bytes 393220
  208.0 4.9 %copy-start.14 = (bf16[128,512]{1,0:T(8,128)(2,1)S(1)}, bf16[128,512]{1,0:T(8,128)(2,1)}, u32[]{:S(2)}) copy-start(bf16[128,512]{1,0:T(8,128)(2,1)} %get-tuple-element.485) | copy-start | bytes 393220
  208.0 4.8 %copy-start.17 = (f32[128]{0:T(128)S(1)}, f32[128]{0:T(128)}, u32[]{:S(2)}) copy-start(f32[128]{0:T(128)} %get-tuple-element.486) | copy-start | bytes 1540
  208.0 4.8 %copy-start.19 = (f32[128]{0:T(128)S(1)}, f32[128]{0:T(128)}, u32[]{:S(2)}) copy-start(f32[128]{0:T(128)} %get-tuple-element.487) | copy-start | bytes 1540
  208.0 4.8 %copy-start.24 = (bf16[512,128]{1,0:T(8,128)(2,1)S(1)}, bf16[512,128]{1,0:T(8,128)(2,1)}, u32[]{:S(2)}) copy-start(bf16[512,128]{1,0:T(8,128)(2,1)} %get-tuple-element.501) | copy-start | bytes 393220
  214.6 1.6 copy-start.15
  225.3 1.6 copy-start.15
  236.0 1.6 copy-start.15
  246.7 1.6 copy-start.15
  255.7 0.7 copy-start.8
  255.7 0.8 copy-start.9
  255.7 0.9 copy-start.20
  256.6 205.8 %all-reduce.7.cloned.1.call-start = ((), (), s32[]{:S(2)}) async-start(), calls=%async_computation.5 | async-start | bytes 1572864 | tf_op jit(solution)/shard_map/psum | solution.py:138
  340.5 2.5 copy-start.7
  345.4 122.1 %copy-start.1 = (bf16[128,64]{0,1:T(8,128)(2,1)S(1)}, bf16[128,64]{0,1:T(8,128)(2,1)}, u32[]{:S(2)}) copy-start(bf16[128,64]{0,1:T(8,128)(2,1)} %param.19) | copy-start | bytes 49156
Sparse Core Ops, SparseCore 0:
  256.7 80.1 all-reduce.8
  339.6 122.8 all-reduce.6
